TPU v7x, 32 devices: a whole 2x2x4 slice. The times are simulated.
32 devices in a mesh: group: 2 (over x), dp: 2 (over core), tensor: 8 (over z, y).
Axes of the slice: x: 2, y: 2, z: 4, core: 2. Of those that a mesh axis runs over, the one named last changes fastest.
Arguments:
- teacher_hidden: bfloat16 [1024, 8192], P(('group', 'dp'), 'tensor'), may hold values from -6 to 6
- teacher_gain: float32 [8192], P('tensor'), may hold values from 0.1 to 1.9
- project_weight: bfloat16 [8192, 3584], P('tensor'), may hold values from -0.0625 to 0.0625
- student_hidden: bfloat16 [1024, 3584], P(('group', 'dp', 'tensor')), may hold values from -6 to 6
- student_gain: float32 [3584], replicated, may hold values from 0.1 to 1.9
- gate_weight: bfloat16 [3584, 9472], P(('group', 'dp'), 'tensor'), may hold values from -0.09375 to 0.09375
- up_weight: bfloat16 [3584, 9472], P(('group', 'dp'), 'tensor'), may hold values from -0.09375 to 0.09375
- down_weight: bfloat16 [9472, 3584], P('tensor', ('group', 'dp')), may hold values from -0.0625 to 0.0625
- owner_map: int32 [64, 1], P(('group', 'dp')), may hold values from 0 to 3; in each aligned block of 16 rows (0 to 15, 16 to 31, ...) at most 8 rows name the same one
- token_ids: int32 [1024], P(('group', 'dp', 'tensor')), may hold values from 0 to 511
- token_counts: int32 [64], P(('group', 'dp')), may hold values from 1 to 16
- id_weight: float32 [512], replicated, may hold values from 0.25 to 4
Outputs:
- student_out: bfloat16 [4, 16, 32, 3584], P(('group', 'dp'), 'tensor')
- down_grad: float32 [3584, 9472], P(('group', 'dp'), 'tensor')
Inputs may be any that keep to these rules, and one draw needn't show every extreme that they name: `owner_map`: of the 16 episodes of one index of group and dp (aligned blocks of 16 rows), at most 8 have the same owner; owner o is index o of group and dp in mesh order.
All inputs are finite; a program needn't handle non-finite values.
Results may differ from a plain program's by a relative error of at most 0.02.
Values may be sent and summed in bfloat16 or wider, within the bound.
A program may use at most 128 MiB of HBM per device.

v0:
```python
import math
import jax
import jax.numpy as jnp
from jax import lax
from jax.sharding import PartitionSpec as P

DT = 8192
EP_LEN = 16
EPSILON = 1e-06


def build_selector(owner_local, owners, capacity):
    owner_list = owner_local[:, 0]
    onehot = (owner_list[:, None] == jnp.arange(owners, dtype=jnp.int32)[None, :]).astype(jnp.int32)
    earlier = jnp.cumsum(onehot, axis=0) - onehot
    rank_list = jnp.sum(earlier * onehot, axis=1)
    target = owner_list * capacity + rank_list
    return (target[None, :] == jnp.arange(owners * capacity, dtype=jnp.int32)[:, None]).astype(
        jnp.bfloat16
    )


def dispatch_rows(selector, values):
    return jnp.einsum("re,pef->prf", selector, values, preferred_element_type=jnp.float32).astype(
        jnp.bfloat16
    )


def dispatch_plain(selector, values):
    return jnp.einsum("re,pe->pr", selector, values, preferred_element_type=jnp.float32).astype(
        jnp.bfloat16
    )


def regroup_rows(payload):
    return (
        lax.all_to_all(payload[0], ("group", "dp"), split_axis=1, concat_axis=1, tiled=True),
        lax.all_to_all(payload[1], ("group", "dp"), split_axis=1, concat_axis=1, tiled=True),
        lax.all_to_all(payload[2], ("group", "dp"), split_axis=1, concat_axis=1, tiled=True),
    )


def teacher_scaling(raw_rows, teacher_gain):
    widened = raw_rows.astype(jnp.float32)
    return (
        jnp.sum(widened * widened, axis=1),
        (widened * teacher_gain[None, :]).astype(jnp.bfloat16),
    )


def local(
    teacher_hidden,
    teacher_gain,
    project_weight,
    student_hidden,
    student_gain,
    gate_weight,
    up_weight,
    down_weight,
    owner_map,
    token_ids,
    token_counts,
    id_weight,
):
    groups = lax.axis_size("group")
    places = lax.axis_size("dp")
    owners = groups * places
    tensors = lax.axis_size("tensor")
    tensor_index = lax.axis_index("tensor")
    episodes = token_counts.shape[0]
    own_span = EP_LEN // tensors
    capacity = max(2, 2 * episodes // owners)
    received = owners * capacity
    student_width = student_hidden.shape[1]
    selector = build_selector(owner_map, owners, capacity)
    id_rows = token_ids.reshape(own_span, episodes)
    looked = jnp.sum(
        jnp.where(
            id_rows[:, :, None] == jnp.arange(id_weight.shape[0], dtype=jnp.int32)[None, None, :],
            id_weight[None, None, :],
            0.0,
        ),
        axis=2,
    )
    position = tensor_index * own_span + jnp.arange(own_span, dtype=jnp.int32)[:, None]
    token_weight = jnp.where(position < token_counts[None, :], looked, 0.0).astype(jnp.bfloat16)
    sent_weight = dispatch_plain(selector, token_weight)
    sent_student = dispatch_rows(
        selector, student_hidden.reshape(own_span, episodes, student_width)
    )
    squares, scaled = teacher_scaling(teacher_hidden, teacher_gain)
    totals = lax.psum(squares, "tensor")
    inverse = lax.rsqrt(totals / DT + EPSILON)
    share_rows = own_span * episodes
    summed = lax.psum_scatter(
        jnp.dot(scaled, project_weight, preferred_element_type=jnp.float32).astype(jnp.bfloat16),
        "tensor",
        scatter_dimension=0,
        tiled=True,
    ).astype(jnp.float32)
    own_inverse = lax.dynamic_slice_in_dim(inverse, tensor_index * share_rows, share_rows, 0)
    projected = (
        (summed * own_inverse[:, None])
        .astype(jnp.bfloat16)
        .reshape(own_span, episodes, student_width)
    )
    arrived = regroup_rows((dispatch_rows(selector, projected), sent_student, sent_weight))
    teacher_mine = arrived[0]
    student_block = arrived[1].reshape(own_span * received, student_width).astype(jnp.float32)
    rescale = lax.rsqrt(jnp.mean(student_block * student_block, axis=1, keepdims=True) + EPSILON)
    normed = (student_block * rescale * student_gain[None, :]).astype(jnp.bfloat16)
    gathered = lax.all_gather(normed, "tensor", axis=0, tiled=True)
    gate_sum = jnp.dot(
        gathered,
        lax.all_gather(gate_weight, ("group", "dp"), axis=0, tiled=True),
        preferred_element_type=jnp.float32,
    )
    up_sum = jnp.dot(
        gathered,
        lax.all_gather(up_weight, ("group", "dp"), axis=0, tiled=True),
        preferred_element_type=jnp.float32,
    )
    activated = (jax.nn.silu(gate_sum) * up_sum).astype(jnp.bfloat16)
    branch = jnp.dot(
        activated,
        lax.all_gather(down_weight, ("group", "dp"), axis=1, tiled=True),
        preferred_element_type=jnp.float32,
    )
    branch_local = lax.psum_scatter(
        branch.astype(jnp.bfloat16), "tensor", scatter_dimension=0, tiled=True
    ).astype(jnp.float32)
    predicted = student_block + branch_local
    student_out = predicted.astype(jnp.bfloat16).reshape(1, own_span, received, student_width)
    difference = predicted - teacher_mine.reshape(-1, student_width).astype(jnp.float32)
    weight_rows = arrived[2].reshape(-1, 1).astype(jnp.float32)
    tokens_all = EP_LEN * episodes * owners
    grad_block = (weight_rows * difference * (1.0 / math.sqrt(tokens_all))).astype(jnp.bfloat16)
    grad_all = lax.all_gather(grad_block, "tensor", axis=0, tiled=True)
    down_grad = lax.psum_scatter(
        jnp.einsum("rc,rh->ch", grad_all, activated, preferred_element_type=jnp.float32).astype(
            jnp.bfloat16
        ),
        ("group", "dp"),
        scatter_dimension=0,
        tiled=True,
    ).astype(jnp.float32)
    return (student_out, down_grad)


def solution(mesh):
    in_specs = (
        P(("group", "dp"), "tensor"),
        P("tensor"),
        P("tensor", None),
        P(("group", "dp", "tensor"), None),
        P(),
        P(("group", "dp"), "tensor"),
        P(("group", "dp"), "tensor"),
        P("tensor", ("group", "dp")),
        P(("group", "dp"), None),
        P(("group", "dp", "tensor")),
        P(("group", "dp")),
        P(),
    )
    out_specs = (P(("group", "dp"), "tensor", None, None), P(("group", "dp"), "tensor"))
    return jax.shard_map(local, mesh=mesh, in_specs=in_specs, out_specs=out_specs, check_vma=False)
```

profile of v0, /device:TPU:0, one launch (start us, length us, event | category | flops | bytes accessed | tf_op | source)
XLA Modules:
  0.0 602.6 jit_solution(13602715377556277750)
XLA Ops:
  7.2 0.8 fusion.17
  8.0 0.8 select_reduce_fusion.1
  8.9 0.7 multiply_add_fusion
  9.5 0.4 fusion
  9.9 0.5 copy.34
  10.4 12.1 %all_to_all.19 = bf16[2,32,3584]{2,0,1:T(2,128)(2,1)S(1)} all-to-all(bf16[2,32,3584]{2,0,1:T(2,128)(2,1)S(1)} %copy.34), channel_id=1, replica_groups=mesh['group'=2,'dp'=2,'tensor'=8] {'group','dp'}, dimensions={1} | all-to-all | bytes 917504 | tf_op jit(solution)/shard_map/all_to_all | solution.py:38
  22.6 0.2 fusion.8
  22.7 0.1 rsqrt.15
  22.8 1.7 fusion.10
  24.6 0.7 all-gather.8.cloned.1.call-update
  25.4 0.7 all-gather.10.cloned.1.call-update
  26.1 0.5 all-gather.12.cloned.1.call-update
  26.7 6.4 %convolution_convert_fusion.2 = bf16[256,3584]{1,0:T(8,128)(2,1)} fusion(bf16[1024,3584]{1,0:T(8,128)(2,1)} %param.14, bf16[256,1024]{1,0:T(8,128)(2,1)S(1)} %copy-done.2, f32[1024]{0:T(1024)S(1)} %copy-done.4), kind=kOutput, calls=%fused_computation.2 | convolution fusion | flops 1880752128 | bytes 9703424 | tf_op jit(solution)/shard_map/dot_general | solution.py:96
  33.1 0.0 reduce-scatter.6.cloned.1.call-start
  33.2 58.1 %all-gather.6.cloned.1.call-done = bf16[512,3584]{1,0:T(8,128)(2,1)} async-done(((bf16[64,3584]{1,0:T(8,128)(2,1)}), bf16[512,3584]{1,0:T(8,128)(2,1)}) %all-gather.6.cloned.1.call-update) | async-done | bytes 3670032 | tf_op jit(solution)/shard_map/all_gather | solution.py:112
  91.3 59.1 %all-gather.8.cloned.1.call-done = bf16[3584,1184]{0,1:T(8,128)(2,1)} async-done(((bf16[896,1184]{0,1:T(8,128)(2,1)}), bf16[3584,1184]{0,1:T(8,128)(2,1)}) %all-gather.8.cloned.1.call-update) | async-done | bytes 8486928 | tf_op jit(solution)/shard_map/all_gather | solution.py:115
  150.4 10.6 %fusion.27 = f32[512,1184]{0,1:T(8,128)} fusion(bf16[512,3584]{1,0:T(8,128)(2,1)} %all-gather.6.cloned.1.call-done, bf16[3584,1184]{0,1:T(8,128)(2,1)} %all-gather.8.cloned.1.call-done), kind=kOutput, calls=%fused_computation.48 | convolution fusion | flops 4345298944 | bytes 14581760 | tf_op jit(solution)/shard_map/dot_general | solution.py:113
  160.9 49.8 %all-gather.10.cloned.1.call-done = bf16[3584,1184]{0,1:T(8,128)(2,1)} async-done(((bf16[896,1184]{0,1:T(8,128)(2,1)}), bf16[3584,1184]{0,1:T(8,128)(2,1)}) %all-gather.10.cloned.1.call-update) | async-done | bytes 8486928 | tf_op jit(solution)/shard_map/all_gather | solution.py:120
  210.7 10.0 %fusion.2 = bf16[512,1184]{0,1:T(8,128)(2,1)S(1)} fusion(bf16[512,3584]{1,0:T(8,128)(2,1)} %all-gather.6.cloned.1.call-done, bf16[3584,1184]{0,1:T(8,128)(2,1)} %all-gather.10.cloned.1.call-done, f32[512,1184]{0,1:T(8,128)} %fusion.27), kind=kOutput, calls=%fused_computation.8 | convolution fusion | flops 4348936192 | bytes 15794176 | tf_op jit(solution)/shard_map/dot_general | solution.py:118
  220.8 50.2 %all-gather.12.cloned.1.call-done = bf16[1184,3584]{1,0:T(8,128)(2,1)} async-done(((bf16[1184,896]{1,0:T(8,128)(2,1)}), bf16[1184,3584]{1,0:T(8,128)(2,1)}) %all-gather.12.cloned.1.call-update) | async-done | bytes 8486928 | tf_op jit(solution)/shard_map/all_gather | solution.py:126
  270.9 9.8 %convolution_convert_fusion.1 = bf16[512,3584]{1,0:T(8,128)(2,1)} fusion(bf16[512,1184]{0,1:T(8,128)(2,1)S(1)} %fusion.2, bf16[1184,3584]{1,0:T(8,128)(2,1)} %all-gather.12.cloned.1.call-done), kind=kOutput, calls=%fused_computation.1 | convolution fusion | flops 4347133952 | bytes 13369344 | tf_op jit(solution)/shard_map/dot_general | solution.py:124
  280.8 0.6 copy-done.5
  281.4 0.1 eq.47
  281.5 0.2 select_reduce_fusion
  281.7 0.2 convolution_convert_fusion.5
  281.9 0.1 all_to_all.13
  281.9 0.6 copy.38
  282.5 3.2 all-to-all-start.1
  285.8 0.2 fusion.4
  286.0 21.6 %psum.7 = f32[256]{0:T(256)S(1)} all-reduce(f32[256]{0:T(256)S(1)} %fusion.4), channel_id=1, replica_groups=mesh['group'=2,'dp'=2,'tensor'=8] {'tensor'}, use_global_device_ids=true, to_apply=%region_7.8 | all-reduce | flops 256 | bytes 2048 | tf_op jit(solution)/shard_map/psum | solution.py:92
  307.5 0.1 dynamic_slice.3
  307.6 33.5 %reduce-scatter.8.cloned.1.call-done = bf16[32,3584]{1,0:T(8,128)(2,1)} async-done(((bf16[256,3584]{1,0:T(8,128)(2,1)}), bf16[32,3584]{1,0:T(8,128)(2,1)}) %reduce-scatter.8.cloned.1.call-update) | async-done | bytes 229392 | tf_op jit(solution)/shard_map/reduce_scatter | solution.py:95
  341.1 1.0 multiply_convert_fusion
  342.2 0.4 fusion.1
  342.6 1.2 copy.40
  343.8 3.5 all-to-all-start.2
  347.3 0.0 all-gather.14.cloned.1.call-start
  347.4 0.1 reshape.72
  347.5 7.9 %all-to-all-done.2 = bf16[2,32,3584]{2,0,1:T(2,128)(2,1)S(1)} async-done(((bf16[2,32,3584]{2,0,1:T(2,128)(2,1)}), bf16[2,32,3584]{2,0,1:T(2,128)(2,1)S(1)}, u32[]{:S(2)}, u32[]{:S(2)}) %all-to-all-start.2) | async-done | bytes 458784 | tf_op jit(solution)/shard_map/all_to_all | solution.py:37
  355.4 69.6 %reduce-scatter.6.cloned.1.call-done = bf16[64,3584]{1,0:T(8,128)(2,1)} async-done(((bf16[512,3584]{1,0:T(8,128)(2,1)}), bf16[64,3584]{1,0:T(8,128)(2,1)}) %reduce-scatter.6.cloned.1.call-update) | async-done | bytes 458768 | tf_op jit(solution)/shard_map/reduce_scatter | solution.py:129
  425.0 2.1 fusion.7
  427.2 0.0 reduce-scatter.10.cloned.1.call-start
  427.3 66.6 %all-gather.14.cloned.1.call-done = bf16[512,3584]{1,0:T(8,128)(2,1)} async-done(((bf16[64,3584]{1,0:T(8,128)(2,1)}), bf16[512,3584]{1,0:T(8,128)(2,1)}) %all-gather.14.cloned.1.call-update) | async-done | bytes 3670032 | tf_op jit(solution)/shard_map/all_gather | solution.py:138
  493.8 8.7 %convolution_convert_fusion = bf16[3584,1184]{0,1:T(8,128)(2,1)} fusion(bf16[512,1184]{0,1:T(8,128)(2,1)S(1)} %fusion.2, bf16[512,3584]{1,0:T(8,128)(2,1)} %all-gather.14.cloned.1.call-done), kind=kOutput, calls=%fused_computation | convolution fusion | flops 4349542400 | bytes 13369344 | tf_op jit(solution)/shard_map/rc,rh->ch/dot_general | solution.py:140
  502.6 12.6 %copy.42 = bf16[3584,1184]{1,0:T(8,128)(2,1)} copy(bf16[3584,1184]{0,1:T(8,128)(2,1)} %convolution_convert_fusion) | data formatting | bytes 16973824
  515.2 75.1 %reduce-scatter.10.cloned.1.call-done = bf16[896,1184]{1,0:T(8,128)(2,1)} async-done(((bf16[3584,1184]{1,0:T(8,128)(2,1)}), bf16[896,1184]{1,0:T(8,128)(2,1)}) %reduce-scatter.10.cloned.1.call-update) | async-done | bytes 2121744
  590.3 3.2 copy.43
  593.5 2.3 convert_element_type.113
  (30 shorter events, 0.4 us)
Async XLA Ops:
  7.2 2.4 copy-start
  7.2 84.1 %all-gather.6.cloned.1.call-start = ((), (), s32[]{:S(2)}) async-start(), calls=%async_computation.6 | async-start | bytes 4128768 | tf_op jit(solution)/shard_map/all_gather | solution.py:112
  22.8 3.9 copy-start.2
  22.8 3.9 copy-start.4
  24.6 125.8 %all-gather.8.cloned.1.call-start = ((), (), s32[]{:S(2)}) async-start(), calls=%async_computation.7 | async-start | bytes 10608640 | tf_op jit(solution)/shard_map/all_gather | solution.py:115
  25.3 185.4 %all-gather.10.cloned.1.call-start = ((), (), s32[]{:S(2)}) async-start(), calls=%async_computation.8 | async-start | bytes 10608640 | tf_op jit(solution)/shard_map/all_gather | solution.py:120
  26.1 244.9 %all-gather.12.cloned.1.call-start = ((), (), s32[]{:S(2)}) async-start(), calls=%async_computation.9 | async-start | bytes 10608640 | tf_op jit(solution)/shard_map/all_gather | solution.py:126
  26.6 314.5 %reduce-scatter.8.cloned.1.call-start = ((), (), s32[]{:S(2)}) async-start(), calls=%async_computation.11 | async-start | bytes 2064384 | tf_op jit(solution)/shard_map/reduce_scatter | solution.py:95
  33.1 391.9 %reduce-scatter.6.cloned.1.call-start = ((), (), s32[]{:S(2)}) async-start(), calls=%async_computation.10 | async-start | bytes 4128768 | tf_op jit(solution)/shard_map/reduce_scatter | solution.py:129
  280.8 0.7 copy-start.5
  280.8 0.7 copy-start.3
  280.8 0.9 copy-start.6
  282.5 61.3 %all-to-all-start.1 = ((bf16[2,4,8]{2,0,1:T(2,128)(2,1)}), bf16[2,4,8]{2,0,1:T(2,128)(2,1)S(1)}, u32[]{:S(2)}, u32[]{:S(2)}) async-start(bf16[2,4,8]{2,0,1:T(2,128)(2,1)} %copy.38), calls=%async_computation.2 | async-start | bytes 4096 | tf_op jit(solution)/shard_map/all_to_all | solution.py:39
  343.8 11.6 %all-to-all-start.2 = ((bf16[2,32,3584]{2,0,1:T(2,128)(2,1)}), bf16[2,32,3584]{2,0,1:T(2,128)(2,1)S(1)}, u32[]{:S(2)}, u32[]{:S(2)}) async-start(bf16[2,32,3584]{2,0,1:T(2,128)(2,1)} %copy.40), calls=%async_computation.4 | async-start | bytes 917504 | tf_op jit(solution)/shard_map/all_to_all | solution.py:37
  347.3 146.5 %all-gather.14.cloned.1.call-start = ((), (), s32[]{:S(2)}) async-start(), calls=%async_computation.12 | async-start | bytes 4128768 | tf_op jit(solution)/shard_map/all_gather | solution.py:138
  427.2 163.1 %reduce-scatter.10.cloned.1.call-start = ((), (), s32[]{:S(2)}) async-start(), calls=%async_computation.13 | async-start | bytes 11468800
  590.3 5.5 copy-start.1
Sparse Core Ops, SparseCore 0:
  24.7 66.5 all-gather.5
  92.8 57.4 all-gather.7
  151.9 58.7 all-gather.9
  212.1 58.7 all-gather.11
  274.3 66.8 reduce-scatter.7
  345.2 79.7 reduce-scatter.5
  427.8 65.9 all-gather.13
  515.3 74.9 reduce-scatter.9
where the time goes:
time: 604 us; the launch traced here: 603 us
  waiting for transfers between devices  472 us (78%)
  matrix products  46.5 us (8%)
  blocking collectives  33.7 us (6%)
  local copies, waits for them, and re-layouts  19.2 us (3%)
  between operations  14.3 us (2%)
  other arithmetic  10.1 us (2%)
  starting transfers between devices  7.01 us (1%)
    unnamed x9, waiting for transfers between devices  77.1 us
    reduce_scatter x1, waiting for transfers between devices, local(): lax.psum_scatter(branch.astype(jnp.bfloat16), 'tensor', scatter_dimension...  69.6 us
    all_gather x1, waiting for transfers between devices, local(): grad_all = lax.all_gather(grad_block, 'tensor', axis=0, tiled=True)  66.6 us
    all_gather x1, waiting for transfers between devices, local(): lax.all_gather(gate_weight, ('group', 'dp'), axis=0, tiled=True)  59.1 us
    all_gather x1, waiting for transfers between devices, local(): gathered = lax.all_gather(normed, 'tensor', axis=0, tiled=True)  58.1 us
    all_gather x1, waiting for transfers between devices, local(): lax.all_gather(down_weight, ('group', 'dp'), axis=1, tiled=True)  50.2 us
    all_gather x1, waiting for transfers between devices, local(): lax.all_gather(up_weight, ('group', 'dp'), axis=0, tiled=True)  49.8 us
    reduce_scatter x1, waiting for transfers between devices, local(): lax.psum_scatter(jnp.dot(scaled, project_weight, preferred_element_type=j...  33.5 us
  transfers between devices with their start and end apart: 10, of which 9 were waited for; matrix products, arithmetic and copies ran while one was open for 7% of the time, Pallas kernels for 0%

commit v1 on v0

--- a/solution.py
+++ b/solution.py
@@ -109,7 +109,14 @@
     student_block = arrived[1].reshape(own_span * received, student_width).astype(jnp.float32)
     rescale = lax.rsqrt(jnp.mean(student_block * student_block, axis=1, keepdims=True) + EPSILON)
     normed = (student_block * rescale * student_gain[None, :]).astype(jnp.bfloat16)
-    gathered = lax.all_gather(normed, "tensor", axis=0, tiled=True)
+    ring = [normed]
+    for hop in range(7):
+        ring.append(lax.ppermute(ring[-1], "tensor", [(dev, (dev + 1) % 8) for dev in range(8)]))
+    gathered = jnp.roll(
+        jnp.concatenate(ring[::-1], axis=0),
+        (lax.axis_index("tensor") + 1) * ring[0].shape[0],
+        axis=0,
+    )
     gate_sum = jnp.dot(
         gathered,
         lax.all_gather(gate_weight, ("group", "dp"), axis=0, tiled=True),

time: 604 us -> 464 us (0.77)
  waiting for transfers between devices: 472 us -> 310 us
  local copies, waits for them, and re-layouts: 19.2 us -> 35.6 us
    ppermute x0 -> x7, waiting for transfers between devices: none -> 81.3 us  [local(): lax.ppermute(ring[-1], 'tensor', [(dev, (dev + 1) % 8) for dev in range(8)])]
    all_gather x1, waiting for transfers between devices: 59.1 us -> 0.01 us  [local(): lax.all_gather(gate_weight, ('group', 'dp'), axis=0, tiled=True)]
    all_gather x1 -> x0, waiting for transfers between devices: 58.1 us -> none  [local(): gathered = lax.all_gather(normed, 'tensor', axis=0, tiled=True)]
    all_gather x1, waiting for transfers between devices: 49.8 us -> 0.01 us  [local(): lax.all_gather(up_weight, ('group', 'dp'), axis=0, tiled=True)]
    reduce_scatter x1, waiting for transfers between devices: 33.5 us -> 0.01 us  [local(): lax.psum_scatter(jnp.dot(scaled, project_weight, preferred_element_type=j...]
    reduce_scatter x1, waiting for transfers between devices: 69.6 us -> 40.1 us  [local(): lax.psum_scatter(branch.astype(jnp.bfloat16), 'tensor', scatter_dimension...]
    unnamed x16 -> x33, local copies, waits for them, and re-layouts: 16.4 us -> 32.1 us
    all_gather x1, waiting for transfers between devices: 50.2 us -> 37.4 us  [local(): lax.all_gather(down_weight, ('group', 'dp'), axis=1, tiled=True)]
  transfers between devices with their start and end apart: 10 -> 16, of which waited for: 9 -> 12; matrix products, arithmetic and copies ran while one was open for 7% -> 14% of each run, Pallas kernels for 0% -> 0%
where the time goes in v1:
time: 464 us; the launch traced here: 463 us
  waiting for transfers between devices  310 us (67%)
  matrix products  48.1 us (10%)
  blocking collectives  35.8 us (8%)
  local copies, waits for them, and re-layouts  35.6 us (8%)
  between operations  15.7 us (3%)
  starting transfers between devices  8.96 us (2%)
  other arithmetic  8.49 us (2%)
    ppermute x7, waiting for transfers between devices, local(): lax.ppermute(ring[-1], 'tensor', [(dev, (dev + 1) % 8) for dev in range(8)])  81.3 us
    unnamed x8, waiting for transfers between devices  77.3 us
    all_gather x1, waiting for transfers between devices, local(): grad_all = lax.all_gather(grad_block, 'tensor', axis=0, tiled=True)  66 us
    reduce_scatter x1, waiting for transfers between devices, local(): lax.psum_scatter(branch.astype(jnp.bfloat16), 'tensor', scatter_dimension...  40.1 us
    all_gather x1, waiting for transfers between devices, local(): lax.all_gather(down_weight, ('group', 'dp'), axis=1, tiled=True)  37.4 us
    unnamed x33, local copies, waits for them, and re-layouts  32.1 us
    psum x1, blocking collectives, local(): totals = lax.psum(squares, 'tensor')  22.3 us
    all_to_all x1, blocking collectives, regroup_rows(): lax.all_to_all(payload[1], ('group', 'dp'), split_axis=1, concat_axis=1,...  13.5 us
  transfers between devices with their start and end apart: 16, of which 12 were waited for; matrix products, arithmetic and copies ran while one was open for 14% of the time, Pallas kernels for 0%

profile of v1, /device:TPU:0, one launch (start us, length us, event | category | flops | bytes accessed | tf_op | source)
XLA Modules:
  0.0 462.7 jit_solution(4166339590388104431)
XLA Ops:
  8.8 0.7 all-gather.7.cloned.1.call-update
  9.6 0.7 all-gather.9.cloned.1.call-update
  10.3 0.7 fusion.20
  11.1 0.8 select_reduce_fusion.1
  13.4 13.5 %all_to_all.19 = bf16[2,32,3584]{2,0,1:T(2,128)(2,1)S(1)} all-to-all(bf16[2,32,3584]{2,0,1:T(2,128)(2,1)S(1)} %copy.34), channel_id=1, replica_groups=mesh['group'=2,'dp'=2,'tensor'=8] {'group','dp'}, dimensions={1} | all-to-all | bytes 917504 | tf_op jit(solution)/shard_map/all_to_all | solution.py:38
  27.4 1.6 collective-permute-start
  29.1 13.7 %collective-permute-done = bf16[64,3584]{1,0:T(8,128)(2,1)S(1)} collective-permute-done((bf16[64,3584]{1,0:T(8,128)(2,1)S(1)}, bf16[64,3584]{1,0:T(8,128)(2,1)S(1)}, u32[]{:S(2)}, u32[]{:S(2)}) %collective-permute-start) | collective-permute-done | bytes 458784 | tf_op jit(solution)/shard_map/ppermute | solution.py:114
  42.7 14.2 %collective-permute-done.1 = bf16[64,3584]{1,0:T(8,128)(2,1)S(1)} collective-permute-done((bf16[64,3584]{1,0:T(8,128)(2,1)S(1)}, bf16[64,3584]{1,0:T(8,128)(2,1)S(1)}, u32[]{:S(2)}, u32[]{:S(2)}) %collective-permute-start.1) | collective-permute-done | bytes 458784 | tf_op jit(solution)/shard_map/ppermute | solution.py:114
  57.0 13.4 %collective-permute-done.2 = bf16[64,3584]{1,0:T(8,128)(2,1)S(1)} collective-permute-done((bf16[64,3584]{1,0:T(8,128)(2,1)S(1)}, bf16[64,3584]{1,0:T(8,128)(2,1)S(1)}, u32[]{:S(2)}, u32[]{:S(2)}) %collective-permute-start.2) | collective-permute-done | bytes 458784 | tf_op jit(solution)/shard_map/ppermute | solution.py:114
  70.4 12.5 %collective-permute-done.3 = bf16[64,3584]{1,0:T(8,128)(2,1)S(1)} collective-permute-done((bf16[64,3584]{1,0:T(8,128)(2,1)S(1)}, bf16[64,3584]{1,0:T(8,128)(2,1)S(1)}, u32[]{:S(2)}, u32[]{:S(2)}) %collective-permute-start.3) | collective-permute-done | bytes 458784 | tf_op jit(solution)/shard_map/ppermute | solution.py:114
  82.9 11.7 %collective-permute-done.4 = bf16[64,3584]{1,0:T(8,128)(2,1)S(1)} collective-permute-done((bf16[64,3584]{1,0:T(8,128)(2,1)S(1)}, bf16[64,3584]{1,0:T(8,128)(2,1)S(1)}, u32[]{:S(2)}, u32[]{:S(2)}) %collective-permute-start.4) | collective-permute-done | bytes 458784 | tf_op jit(solution)/shard_map/ppermute | solution.py:114
  94.6 11.3 %collective-permute-done.5 = bf16[64,3584]{1,0:T(8,128)(2,1)} collective-permute-done((bf16[64,3584]{1,0:T(8,128)(2,1)S(1)}, bf16[64,3584]{1,0:T(8,128)(2,1)}, u32[]{:S(2)}, u32[]{:S(2)}) %collective-permute-start.5) | collective-permute-done | bytes 458784 | tf_op jit(solution)/shard_map/ppermute | solution.py:114
  105.8 6.7 %convolution_convert_fusion.2 = bf16[256,3584]{1,0:T(8,128)(2,1)} fusion(bf16[1024,3584]{1,0:T(8,128)(2,1)} %param.14, bf16[256,1024]{1,0:T(8,128)(2,1)} %param.12, f32[1024]{0:T(1024)S(1)} %copy-done.5), kind=kOutput, calls=%fused_computation.2 | convolution fusion | flops 1880752128 | bytes 9703424 | tf_op jit(solution)/shard_map/dot_general | solution.py:96
  112.8 4.5 collective-permute-done.6
  117.3 1.9 constant_dynamic-update-slice_fusion.15
  119.2 1.8 constant_dynamic-update-slice_fusion.14
  121.0 0.8 constant_dynamic-update-slice_fusion.13
  121.8 0.8 constant_dynamic-update-slice_fusion.12
  122.7 0.8 constant_dynamic-update-slice_fusion.11
  123.5 0.8 constant_dynamic-update-slice_fusion.10
  124.3 0.8 constant_dynamic-update-slice_fusion.9
  125.1 0.8 constant_dynamic-update-slice_fusion.8
  125.9 1.8 constant_dynamic-update-slice_fusion.7
  127.7 1.9 constant_dynamic-update-slice_fusion.6
  129.7 0.8 constant_dynamic-update-slice_fusion.5
  130.5 0.8 constant_dynamic-update-slice_fusion.4
  131.3 0.8 constant_dynamic-update-slice_fusion.3
  132.1 0.8 constant_dynamic-update-slice_fusion.2
  132.9 0.8 constant_dynamic-update-slice_fusion.1
  133.7 0.8 constant_dynamic-update-slice_fusion
  134.5 10.6 %fusion.4 = f32[512,1184]{0,1:T(8,128)} fusion(bf16[3584,1184]{0,1:T(8,128)(2,1)} %all-gather.5.cloned.1.call-done, bf16[1024,3584]{1,0:T(8,128)(2,1)} %constant_dynamic-update-slice_fusion, s32[]{:T(128)S(6)} %select_n.25), kind=kOutput, calls=%fused_computation.9 | convolution fusion | flops 4345298944 | bytes 14581764 | tf_op jit(solution)/shard_map/dot_general | solution.py:120
  145.1 11.3 %multiply_convert_fusion = bf16[512,1184]{0,1:T(8,128)(2,1)S(1)} fusion(f32[512,1184]{0,1:T(8,128)} %fusion.4, bf16[3584,1184]{0,1:T(8,128)(2,1)} %all-gather.7.cloned.1.call-done, bf16[1024,3584]{1,0:T(8,128)(2,1)} %constant_dynamic-update-slice_fusion, s32[]{:T(128)S(6)} %select_n.25), kind=kOutput, calls=%fused_computation.11 | convolution fusion | flops 4348936192 | bytes 15794180 | tf_op jit(solution)/shard_map/dot_general | solution.py:125
  156.5 37.4 %all-gather.9.cloned.1.call-done = bf16[1184,3584]{1,0:T(8,128)(2,1)} async-done(((bf16[1184,896]{1,0:T(8,128)(2,1)}), bf16[1184,3584]{1,0:T(8,128)(2,1)}) %all-gather.9.cloned.1.call-update) | async-done | bytes 8486928 | tf_op jit(solution)/shard_map/all_gather | solution.py:133
  193.8 9.8 %convolution_convert_fusion.1 = bf16[512,3584]{1,0:T(8,128)(2,1)} fusion(bf16[512,1184]{0,1:T(8,128)(2,1)S(1)} %multiply_convert_fusion, bf16[1184,3584]{1,0:T(8,128)(2,1)} %all-gather.9.cloned.1.call-done), kind=kOutput, calls=%fused_computation.1 | convolution fusion | flops 4347133952 | bytes 13369344 | tf_op jit(solution)/shard_map/dot_general | solution.py:131
  204.8 3.2 all-to-all-start.1
  208.1 22.3 %psum.7 = f32[256]{0:T(256)S(1)} all-reduce(f32[256]{0:T(256)S(1)} %fusion.7), channel_id=1, replica_groups=mesh['group'=2,'dp'=2,'tensor'=8] {'tensor'}, use_global_device_ids=true, to_apply=%region_7.8 | all-reduce | flops 256 | bytes 2048 | tf_op jit(solution)/shard_map/psum | solution.py:92
  230.5 1.1 multiply_convert_fusion.1
  231.9 1.2 copy.40
  233.2 3.5 all-to-all-start.2
  236.8 7.9 %all-to-all-done.2 = bf16[2,32,3584]{2,0,1:T(2,128)(2,1)S(1)} async-done(((bf16[2,32,3584]{2,0,1:T(2,128)(2,1)}), bf16[2,32,3584]{2,0,1:T(2,128)(2,1)S(1)}, u32[]{:S(2)}, u32[]{:S(2)}) %all-to-all-start.2) | async-done | bytes 458784 | tf_op jit(solution)/shard_map/all_to_all | solution.py:37
  244.8 40.1 %reduce-scatter.6.cloned.1.call-done = bf16[64,3584]{1,0:T(8,128)(2,1)} async-done(((bf16[512,3584]{1,0:T(8,128)(2,1)}), bf16[64,3584]{1,0:T(8,128)(2,1)}) %reduce-scatter.6.cloned.1.call-update) | async-done | bytes 458768 | tf_op jit(solution)/shard_map/reduce_scatter | solution.py:136
  284.9 2.1 fusion.10
  287.4 66.0 %all-gather.11.cloned.1.call-done = bf16[512,3584]{1,0:T(8,128)(2,1)} async-done(((bf16[64,3584]{1,0:T(8,128)(2,1)}), bf16[512,3584]{1,0:T(8,128)(2,1)}) %all-gather.11.cloned.1.call-update) | async-done | bytes 3670032 | tf_op jit(solution)/shard_map/all_gather | solution.py:145
  353.4 8.8 %convolution_convert_fusion = bf16[3584,1184]{0,1:T(8,128)(2,1)} fusion(bf16[512,1184]{0,1:T(8,128)(2,1)S(1)} %multiply_convert_fusion, bf16[512,3584]{1,0:T(8,128)(2,1)} %all-gather.11.cloned.1.call-done), kind=kOutput, calls=%fused_computation | convolution fusion | flops 4349542400 | bytes 13369344 | tf_op jit(solution)/shard_map/rc,rh->ch/dot_general | solution.py:147
  362.2 12.6 %copy.42 = bf16[3584,1184]{1,0:T(8,128)(2,1)} copy(bf16[3584,1184]{0,1:T(8,128)(2,1)} %convolution_convert_fusion) | data formatting | bytes 16973824
  374.8 75.2 %reduce-scatter.10.cloned.1.call-done = bf16[896,1184]{1,0:T(8,128)(2,1)} async-done(((bf16[3584,1184]{1,0:T(8,128)(2,1)}), bf16[896,1184]{1,0:T(8,128)(2,1)}) %reduce-scatter.10.cloned.1.call-update) | async-done | bytes 2121744
  450.0 3.1 copy.43
  453.1 2.3 convert_element_type.113
  (59 shorter events, 5.4 us)
Async XLA Ops:
  8.0 4.6 copy-start
  8.0 19.2 %copy-start.3 = (f32[3584]{0:T(1024)S(1)}, f32[3584]{0:T(1024)}, u32[]{:S(2)}) copy-start(f32[3584]{0:T(1024)} %param.16) | copy-start | bytes 43012
  8.0 97.8 %copy-start.5 = (f32[1024]{0:T(1024)S(1)}, f32[1024]{0:T(1024)}, u32[]{:S(2)}) copy-start(f32[1024]{0:T(1024)} %param.13) | copy-start | bytes 12292
  8.0 126.4 %all-gather.5.cloned.1.call-start = ((), (), s32[]{:S(2)}) async-start(), calls=%async_computation.6 | async-start | bytes 10608640 | tf_op jit(solution)/shard_map/all_gather | solution.py:122
  8.8 136.3 %all-gather.7.cloned.1.call-start = ((), (), s32[]{:S(2)}) async-start(), calls=%async_computation.7 | async-start | bytes 10608640 | tf_op jit(solution)/shard_map/all_gather | solution.py:127
  9.5 184.3 %all-gather.9.cloned.1.call-start = ((), (), s32[]{:S(2)}) async-start(), calls=%async_computation.8 | async-start | bytes 10608640 | tf_op jit(solution)/shard_map/all_gather | solution.py:133
  10.3 220.2 %reduce-scatter.8.cloned.1.call-start = ((), (), s32[]{:S(2)}) async-start(), calls=%async_computation.10 | async-start | bytes 2064384 | tf_op jit(solution)/shard_map/reduce_scatter | solution.py:95
  27.4 15.3 %collective-permute-start = (bf16[64,3584]{1,0:T(8,128)(2,1)S(1)}, bf16[64,3584]{1,0:T(8,128)(2,1)S(1)}, u32[]{:S(2)}, u32[]{:S(2)}) collective-permute-start(bf16[64,3584]{1,0:T(8,128)(2,1)S(1)} %fusion.13), channel_id=1, source_target_pairs={{0,1},{1,2},{2,3},{3,4},{4,5},{5,6},{6,7},{7,0},{8,9},{9,10},{10,1... | collective-permute-start | bytes 1376264 | tf_op jit(solution)/shard_map/ppermute | solution.py:114
  42.7 14.2 %collective-permute-start.1 = (bf16[64,3584]{1,0:T(8,128)(2,1)S(1)}, bf16[64,3584]{1,0:T(8,128)(2,1)S(1)}, u32[]{:S(2)}, u32[]{:S(2)}) collective-permute-start(bf16[64,3584]{1,0:T(8,128)(2,1)S(1)} %collective-permute-done), channel_id=1, source_target_pairs={{0,1},{1,2},{2,3},{3,4},{4,5},{5,6},{6,7},{7,0},{8,9},{9,10},{10,1... | collective-permute-start | bytes 1376264 | tf_op jit(solution)/shard_map/ppermute | solution.py:114
  57.0 13.4 %collective-permute-start.2 = (bf16[64,3584]{1,0:T(8,128)(2,1)S(1)}, bf16[64,3584]{1,0:T(8,128)(2,1)S(1)}, u32[]{:S(2)}, u32[]{:S(2)}) collective-permute-start(bf16[64,3584]{1,0:T(8,128)(2,1)S(1)} %collective-permute-done.1), channel_id=1, source_target_pairs={{0,1},{1,2},{2,3},{3,4},{4,5},{5,6},{6,7},{7,0},{8,9},{9,10},{10,1... | collective-permute-start | bytes 1376264 | tf_op jit(solution)/shard_map/ppermute | solution.py:114
  70.4 12.5 %collective-permute-start.3 = (bf16[64,3584]{1,0:T(8,128)(2,1)S(1)}, bf16[64,3584]{1,0:T(8,128)(2,1)S(1)}, u32[]{:S(2)}, u32[]{:S(2)}) collective-permute-start(bf16[64,3584]{1,0:T(8,128)(2,1)S(1)} %collective-permute-done.2), channel_id=1, source_target_pairs={{0,1},{1,2},{2,3},{3,4},{4,5},{5,6},{6,7},{7,0},{8,9},{9,10},{10,1... | collective-permute-start | bytes 1376264 | tf_op jit(solution)/shard_map/ppermute | solution.py:114
  82.9 11.7 %collective-permute-start.4 = (bf16[64,3584]{1,0:T(8,128)(2,1)S(1)}, bf16[64,3584]{1,0:T(8,128)(2,1)S(1)}, u32[]{:S(2)}, u32[]{:S(2)}) collective-permute-start(bf16[64,3584]{1,0:T(8,128)(2,1)S(1)} %collective-permute-done.3), channel_id=1, source_target_pairs={{0,1},{1,2},{2,3},{3,4},{4,5},{5,6},{6,7},{7,0},{8,9},{9,10},{10,1... | collective-permute-start | bytes 1376264 | tf_op jit(solution)/shard_map/ppermute | solution.py:114
  94.6 11.3 %collective-permute-start.5 = (bf16[64,3584]{1,0:T(8,128)(2,1)S(1)}, bf16[64,3584]{1,0:T(8,128)(2,1)}, u32[]{:S(2)}, u32[]{:S(2)}) collective-permute-start(bf16[64,3584]{1,0:T(8,128)(2,1)S(1)} %collective-permute-done.4), channel_id=1, source_target_pairs={{0,1},{1,2},{2,3},{3,4},{4,5},{5,6},{6,7},{7,0},{8,9},{9,10},{10,1... | collective-permute-start | bytes 1376264 | tf_op jit(solution)/shard_map/ppermute | solution.py:114
  105.8 11.5 %collective-permute-start.6 = (bf16[64,3584]{1,0:T(8,128)(2,1)}, bf16[64,3584]{1,0:T(8,128)(2,1)}, u32[]{:S(2)}, u32[]{:S(2)}) collective-permute-start(bf16[64,3584]{1,0:T(8,128)(2,1)} %collective-permute-done.5), channel_id=1, source_target_pairs={{0,1},{1,2},{2,3},{3,4},{4,5},{5,6},{6,7},{7,0},{8,9},{9,10},{10,1... | collective-permute-start | bytes 1376264 | tf_op jit(solution)/shard_map/ppermute | solution.py:114
  112.5 172.4 %reduce-scatter.6.cloned.1.call-start = ((), (), s32[]{:S(2)}) async-start(), calls=%async_computation.9 | async-start | bytes 4128768 | tf_op jit(solution)/shard_map/reduce_scatter | solution.py:136
  156.4 47.2 %copy-start.6 = (s32[32]{0:T(128)S(1)}, s32[32]{0:T(128)}, u32[]{:S(2)}) copy-start(s32[32]{0:T(128)} %param.21) | copy-start | bytes 388
  156.4 47.3 %copy-start.4 = (f32[512]{0:T(512)S(1)}, f32[512]{0:T(512)}, u32[]{:S(2)}) copy-start(f32[512]{0:T(512)} %param.23) | copy-start | bytes 6148
  156.5 47.5 %copy-start.7 = (s32[16]{0:T(128)S(1)}, s32[16]{0:T(128)}, u32[]{:S(2)}) copy-start(s32[16]{0:T(128)} %param.22) | copy-start | bytes 196
  156.5 51.5 %copy-start.2 = (bf16[256,1024]{1,0:T(8,128)(2,1)S(1)}, bf16[256,1024]{1,0:T(8,128)(2,1)}, u32[]{:S(2)}) copy-start(bf16[256,1024]{1,0:T(8,128)(2,1)} %param.12) | copy-start | bytes 1572868
  204.8 28.4 %all-to-all-start.1 = ((bf16[2,4,8]{2,0,1:T(2,128)(2,1)}), bf16[2,4,8]{2,0,1:T(2,128)(2,1)S(1)}, u32[]{:S(2)}, u32[]{:S(2)}) async-start(bf16[2,4,8]{2,0,1:T(2,128)(2,1)} %copy.38), calls=%async_computation.2 | async-start | bytes 4096 | tf_op jit(solution)/shard_map/all_to_all | solution.py:39
  233.2 11.6 %all-to-all-start.2 = ((bf16[2,32,3584]{2,0,1:T(2,128)(2,1)}), bf16[2,32,3584]{2,0,1:T(2,128)(2,1)S(1)}, u32[]{:S(2)}, u32[]{:S(2)}) async-start(bf16[2,32,3584]{2,0,1:T(2,128)(2,1)} %copy.40), calls=%async_computation.4 | async-start | bytes 917504 | tf_op jit(solution)/shard_map/all_to_all | solution.py:37
  236.7 116.7 %all-gather.11.cloned.1.call-start = ((), (), s32[]{:S(2)}) async-start(), calls=%async_computation.11 | async-start | bytes 4128768 | tf_op jit(solution)/shard_map/all_gather | solution.py:145
  287.1 162.9 %reduce-scatter.10.cloned.1.call-start = ((), (), s32[]{:S(2)}) async-start(), calls=%async_computation.12 | async-start | bytes 11468800
  374.8 80.6 %copy-start.1 = (bf16[32,3584]{1,0:T(8,128)(2,1)S(1)}, bf16[32,3584]{1,0:T(8,128)(2,1)}, u32[]{:S(2)}) copy-start(bf16[32,3584]{1,0:T(8,128)(2,1)} %param.15) | copy-start | bytes 688132
Sparse Core Ops, SparseCore 0:
  10.4 62.3 all-gather.4
  74.4 59.0 all-gather.6
  135.0 58.7 all-gather.8
  374.9 75.0 reduce-scatter.9
Sparse Core Ops, SparseCore 1:
  112.6 67.1 reduce-scatter.7
  203.8 81.1 reduce-scatter.5
  287.6 65.8 all-gather.10
